TPU v7x, 32 devices: a whole 2x2x4 slice. The times are simulated.
32 devices in a mesh: dp: 8 (over z, x), zero: 4 (over y, core).
Axes of the slice: x: 2, y: 2, z: 4, core: 2. Of those that a mesh axis runs over, the one named last changes fastest.
Arguments:
- tokens: bfloat16 [64, 1024, 768], P('zero', 'dp'), may hold values from -6 to 6
- loss_sensitivity: bfloat16 [32, 1024, 768], P(('dp', 'zero')), may hold values from -6 to 6
- lengths: int32 [64], replicated, may hold values from 0 to 1024, as said below
- holder_sequence_list: int32 [64], replicated, may hold values from 0 to 63, as said below
- master: float32 [3768320], P('zero')
- moment_one: float32 [3768320], P('zero'), may hold values from -18 to 18
- moment_two: float32 [3768320], P('zero'), may hold values from 1 to 1000
- adam_rates: float32 [2], replicated, may hold values from 0.05 to 0.2
- iteration_tally: int32 [1], replicated, may hold values from 1 to 8
Outputs:
- tokens_out: bfloat16 [64, 1024, 768], P('zero', 'dp')
- grad_tokens: bfloat16 [64, 1024, 768], P('zero', 'dp')
- new_master: float32 [3768320], replicated
- grads: float32 [3768320], P('zero')
- moment_one_out: float32 [3768320], P('zero')
- moment_two_out: float32 [3768320], P('zero')
Inputs may be any that keep to these rules, and one draw needn't show every extreme that they name: A permutation of the sequences. Slot i lies on the device whose index along dp+zero is i // 2, and holder_sequence_list[i] is one of the 64 / 4 sequences of that device's zero index (sequences z * 64 / 4 onward for zero index z). The two sequences of slots 2j and 2j + 1 have lengths summing to exactly 1024; in some pack one of them has 1024 tokens and the other none.
All inputs are finite; a program needn't handle non-finite values.
Results may differ from a plain program's by a relative error of at most 0.002.
The roundings to bfloat16 on the way count: a program that leaves them out, or rounds other values in their place, can miss the bound.
Values may be sent and summed in bfloat16 or wider, within the bound.
No kernel may reach another device: no remote copies, remote signals or barrier semaphores. Data moves between devices by JAX's collectives and lax.ppermute only.
A program may use at most 256 MiB of HBM per device.

v0:
```python
from functools import partial
import jax
import jax.numpy as jnp
from jax import lax
from jax.sharding import PartitionSpec as P

D = 768
HEADS = 24
HEADDIM = 64
STATE = 128
CONV = 4
SPAN = 256
INNER = 1536
XBC = 1792
PROJ = 3352
EXACT_MATMUL = lax.Precision.HIGHEST
EPS_NORM = 1e-05
BETA_ONE = 0.9
BETA_TWO = 0.95
EPS_ADAM = 1e-08


def padded_slot(amount):
    return (amount + 127) // 128 * 128


def unpack(linear_coefficient_list):
    piece_sizes = [D, D * PROJ, CONV * XBC, XBC, HEADS, HEADS, HEADS, INNER, INNER * D]
    pieces = []
    offset = 0
    for amount in piece_sizes:
        pieces.append(linear_coefficient_list[offset : offset + amount])
        offset = offset + padded_slot(amount)
    (
        norm_gain,
        input_weight_t,
        conv_w,
        conv_b,
        dt_bias,
        a_log,
        d_skip,
        gated_gain,
        emitting_matrix,
    ) = pieces
    return (
        norm_gain,
        input_weight_t.reshape(PROJ, D),
        conv_w.reshape(CONV, XBC),
        conv_b,
        dt_bias,
        a_log,
        d_skip,
        gated_gain,
        emitting_matrix.reshape(INNER, D),
    )


def pre_norm(values, gain):
    return values * lax.rsqrt(jnp.mean(values * values, axis=-1, keepdims=True) + EPS_NORM) * gain


def causal_conv(conv_in, conv_w, conv_b, segment):
    seq_len = conv_in.shape[1]
    padded = jnp.pad(conv_in, ((0, 0), (CONV - 1, 0), (0, 0)))
    seg_padded = jnp.pad(segment, ((0, 0), (CONV - 1, 0)), constant_values=-1.0)
    summed = conv_b + jnp.zeros_like(conv_in)
    for offset in range(CONV):
        same_seg = (seg_padded[:, offset : offset + seq_len] == segment).astype(jnp.float32)[
            ..., None
        ]
        summed = summed + conv_w[offset] * (padded[:, offset : offset + seq_len] * same_seg)
    return summed


def span_scan(x_heads, dt_pos, decay_rate, b_rows, c_rows, segment):
    batch_size, seq_len, head_count, head_width = x_heads.shape
    block_count = seq_len // SPAN

    def split_blocks(values):
        shaped = values.reshape((batch_size, block_count, SPAN) + values.shape[2:])
        return jnp.moveaxis(shaped, 1, 0)

    causal = jnp.arange(SPAN)[:, None] >= jnp.arange(SPAN)[None, :]

    def advance(carried_pair, block_in):
        carried, last_seg = carried_pair
        x_blk, dt_blk, b_blk, c_blk, membership_tile = block_in
        dt_cols = jnp.swapaxes(dt_blk, 1, 2)
        cum_blk = jnp.cumsum(dt_cols * decay_rate[None, :, None], axis=2)
        differ = cum_blk[:, :, :, None] - cum_blk[:, :, None, :]
        same_seg = membership_tile[:, :, None] == membership_tile[:, None, :]
        allowed = jnp.logical_and(causal[None], same_seg)[:, None]
        weights_in = jnp.exp(jnp.where(allowed, differ, -jnp.inf))
        gram_blk = jnp.einsum("stn,srn->str", c_blk, b_blk, precision=EXACT_MATMUL)
        mixing = gram_blk[:, None] * weights_in * dt_cols[:, :, None, :]
        inside = jnp.einsum("shtr,srhp->sthp", mixing, x_blk, precision=EXACT_MATMUL)
        from_state = jnp.einsum("stn,shpn->sthp", c_blk, carried, precision=EXACT_MATMUL)
        from_state = from_state * jnp.swapaxes(jnp.exp(cum_blk), 1, 2)[..., None]
        keep_state = (membership_tile == last_seg[:, None]).astype(jnp.float32)
        from_state = from_state * keep_state[:, :, None, None]
        cum_end = cum_blk[:, :, -1]
        end_seg = membership_tile[:, -1]
        in_last = (membership_tile == end_seg[:, None]).astype(jnp.float32)
        carry_weight = jnp.exp(cum_end[:, :, None] - cum_blk) * dt_cols * in_last[:, None, :]
        added_state = jnp.einsum(
            "srn,shr,srhp->shpn", b_blk, carry_weight, x_blk, precision=EXACT_MATMUL
        )
        carry_scale = jnp.exp(cum_end) * (end_seg == last_seg).astype(jnp.float32)[:, None]
        carried = carried * carry_scale[:, :, None, None] + added_state
        return ((carried, end_seg), inside + from_state)

    initial = (
        jnp.zeros((batch_size, head_count, head_width, b_rows.shape[-1]), jnp.float32),
        jnp.zeros((batch_size,), jnp.float32),
    )
    final_pair, outputs = lax.scan(
        jax.checkpoint(advance),
        initial,
        (
            split_blocks(x_heads),
            split_blocks(dt_pos),
            split_blocks(b_rows),
            split_blocks(c_rows),
            split_blocks(segment),
        ),
    )
    return jnp.moveaxis(outputs, 0, 1).reshape(batch_size, seq_len, head_count, head_width)


def mixer_branch(input_projection, conv_w, conv_b, dt_bias, a_log, d_skip, gated_gain, segment):
    batch_size, seq_len = (input_projection.shape[0], input_projection.shape[1])
    gate_z = input_projection[..., :INNER]
    conv_in = input_projection[..., INNER : INNER + XBC]
    dt_raw = input_projection[..., INNER + XBC :]
    conv_out = jax.nn.silu(causal_conv(conv_in, conv_w, conv_b, segment))
    x_heads = conv_out[..., :INNER].reshape(batch_size, seq_len, HEADS, HEADDIM)
    b_rows = conv_out[..., INNER : INNER + STATE]
    c_rows = conv_out[..., INNER + STATE :]
    dt_pos = jax.nn.softplus(dt_raw + dt_bias)
    decay_rate = -jnp.exp(a_log)
    scanned = (
        span_scan(x_heads, dt_pos, decay_rate, b_rows, c_rows, segment) + d_skip[:, None] * x_heads
    )
    gated_out = scanned.reshape(batch_size, seq_len, INNER) * jax.nn.silu(gate_z)
    return (
        gated_out
        * lax.rsqrt(jnp.mean(gated_out * gated_out, axis=-1, keepdims=True) + EPS_NORM)
        * gated_gain
    )


def adam_update(weights, first_moment, second_moment, gradient, adam_rates, iteration_tally):
    steps_f = iteration_tally[0].astype(jnp.float32)
    first_next = BETA_ONE * first_moment + (1.0 - BETA_ONE) * gradient
    second_next = BETA_TWO * second_moment + (1.0 - BETA_TWO) * gradient * gradient
    first_hat = first_next / (1.0 - jnp.power(BETA_ONE, steps_f))
    second_hat = second_next / (1.0 - jnp.power(BETA_TWO, steps_f))
    updated = weights - adam_rates[0] * (
        first_hat / (jnp.sqrt(second_hat) + EPS_ADAM) + adam_rates[1] * weights
    )
    return (updated, first_next, second_next)


def on_device(
    tokens,
    loss_sensitivity,
    lengths,
    holder_sequence_list,
    master,
    moment_one,
    moment_two,
    adam_rates,
    iteration_tally,
):
    group_devices = lax.axis_size("zero")
    data_devices = lax.axis_size("dp")
    zero_index = lax.axis_index("zero")
    dp_index = lax.axis_index("dp")
    pack_count = loss_sensitivity.shape[0]
    slot_count = 2 * pack_count
    seq_len = loss_sensitivity.shape[1]
    model_width = loss_sensitivity.shape[2]
    group_seqs = tokens.shape[0]
    full_weights = lax.all_gather(master.astype(jnp.bfloat16), "zero", axis=0, tiled=True)
    (
        norm_gain,
        input_weight_t,
        conv_w,
        conv_b,
        dt_bias,
        a_log,
        d_skip,
        gated_gain,
        emitting_matrix,
    ) = unpack(full_weights)
    small_f = [
        piece.astype(jnp.float32) for piece in (conv_w, conv_b, dt_bias, a_log, d_skip, gated_gain)
    ]
    norm_gain_f = norm_gain.astype(jnp.float32)
    arranged_order = holder_sequence_list.reshape(data_devices, group_devices, slot_count)
    group_order = lax.dynamic_index_in_dim(arranged_order, zero_index, 1, keepdims=False).reshape(
        -1
    )
    local_ids = group_order - zero_index * group_seqs
    dealt_rows = jnp.take(tokens, local_ids, axis=0)
    local_tok = lax.all_to_all(dealt_rows, "dp", split_axis=0, concat_axis=1, tiled=True)
    my_seqs = lax.dynamic_slice_in_dim(group_order, dp_index * slot_count, slot_count)
    my_lengths = jnp.take(lengths, my_seqs)
    bounds = my_lengths.reshape(pack_count, 2)[:, 0]
    positions = jnp.arange(seq_len, dtype=jnp.int32)
    later_part = positions[None, :] >= bounds[:, None]
    pack_ids = jnp.arange(pack_count, dtype=jnp.int32)[:, None]
    source = jnp.where(
        later_part,
        (2 * pack_ids + 1) * seq_len + positions[None, :] - bounds[:, None],
        2 * pack_ids * seq_len + positions[None, :],
    )
    segment = later_part.astype(jnp.float32)
    slot_rows = local_tok.reshape(slot_count * seq_len, model_width)
    packed_tok = jnp.take(slot_rows, source.reshape(-1), axis=0).reshape(
        pack_count, seq_len, model_width
    )
    place_numbering = jnp.arange(slot_count, dtype=jnp.int32)
    shift_by = jnp.where(place_numbering % 2 == 1, jnp.repeat(bounds, 2), 0)
    within = positions[None, :] + shift_by[:, None]
    unpack_rows = (place_numbering // 2)[:, None] * seq_len + jnp.minimum(within, seq_len - 1)
    slot_live = (positions[None, :] < my_lengths[:, None]).astype(jnp.float32)[..., None]

    def to_slots(values):
        flat_rows = values.reshape(pack_count * seq_len, values.shape[2])
        picked = jnp.take(flat_rows, unpack_rows.reshape(-1), axis=0)
        return picked.reshape(slot_count, seq_len, values.shape[2]) * slot_live

    tokens_f = packed_tok.astype(jnp.float32)
    normalized, norm_pull = jax.vjp(pre_norm, tokens_f, norm_gain_f)
    normalized_rows = normalized.astype(jnp.bfloat16)
    input_projection = jnp.einsum(
        "mgv,bv->mgb", normalized_rows, input_weight_t, preferred_element_type=jnp.float32
    )
    mixer_output, mix_pull = jax.vjp(
        partial(mixer_branch, segment=segment), input_projection, *small_f
    )
    mixer_output_rows = mixer_output.astype(jnp.bfloat16)
    mixer_path = jnp.einsum(
        "ocr,rb->ocb", mixer_output_rows, emitting_matrix, preferred_element_type=jnp.float32
    )
    result = (local_tok.astype(jnp.float32) + to_slots(mixer_path)).astype(jnp.bfloat16)
    cot_f = loss_sensitivity.astype(jnp.float32)
    grad_out_weight = jnp.einsum(
        "uir,uin->rn", mixer_output_rows, loss_sensitivity, preferred_element_type=jnp.float32
    )
    grad_mixed = jnp.einsum(
        "nsa,wa->nsw", loss_sensitivity, emitting_matrix, preferred_element_type=jnp.float32
    )
    grad_proj, grad_conv_w, grad_conv_b, grad_dt_bias, grad_a_log, grad_d_skip, grad_gated = (
        mix_pull(grad_mixed)
    )
    grad_projection_rows = grad_proj.astype(jnp.bfloat16)
    grad_in_weight_t = jnp.einsum(
        "pvr,pvy->ry", grad_projection_rows, normalized_rows, preferred_element_type=jnp.float32
    )
    grad_normed = jnp.einsum(
        "ept,tb->epb", grad_projection_rows, input_weight_t, preferred_element_type=jnp.float32
    )
    grad_tok, grad_norm_gain = norm_pull(grad_normed)
    grad_input = to_slots(cot_f + grad_tok).astype(jnp.bfloat16)
    back_out, back_grad = (
        lax.all_to_all(result, "dp", split_axis=1, concat_axis=0, tiled=True),
        lax.all_to_all(grad_input, "dp", split_axis=1, concat_axis=0, tiled=True),
    )
    restore = jnp.zeros_like(local_ids).at[local_ids].set(jnp.arange(group_seqs, dtype=jnp.int32))
    tokens_out = jnp.take(back_out, restore, axis=0)
    grad_tokens = jnp.take(back_grad, restore, axis=0)
    vector_len = master.shape[0] * group_devices
    used = [
        grad_norm_gain,
        grad_in_weight_t.reshape(-1),
        grad_conv_w.reshape(-1),
        grad_conv_b,
        grad_dt_bias,
        grad_a_log,
        grad_d_skip,
        grad_gated,
        grad_out_weight.reshape(-1),
    ]
    laid = [jnp.pad(piece, (0, padded_slot(piece.shape[0]) - piece.shape[0])) for piece in used]
    used_len = sum((piece.shape[0] for piece in laid))
    flat_grad = jnp.concatenate(laid + [jnp.zeros((vector_len - used_len,), jnp.float32)])
    grad_shard = lax.psum_scatter(flat_grad, "zero", scatter_dimension=0, tiled=True)
    grad_shard = lax.psum(grad_shard, "dp")
    new_shard, first_next, second_next = adam_update(
        master, moment_one, moment_two, grad_shard, adam_rates, iteration_tally
    )
    new_master = lax.all_gather(new_shard, "zero", axis=0, tiled=True)
    return (tokens_out, grad_tokens, new_master, grad_shard, first_next, second_next)


def solution(mesh):
    return jax.shard_map(
        on_device,
        mesh=mesh,
        in_specs=(
            P("zero", "dp", None),
            P(("dp", "zero"), None, None),
            P(),
            P(),
            P("zero"),
            P("zero"),
            P("zero"),
            P(),
            P(),
        ),
        out_specs=(
            P("zero", "dp", None),
            P("zero", "dp", None),
            P(),
            P("zero"),
            P("zero"),
            P("zero"),
        ),
        check_vma=False,
    )
```

profile of v0, /device:TPU:0, one launch (start us, length us, event | category | flops | bytes accessed | tf_op | source)
XLA Modules:
  0.0 1918.3 jit_solution(2939030028046940159)
XLA Ops:
  18.1 7.3 all-to-all-start
  27.2 68.9 %all-to-all-done = bf16[16,128,768]{2,1,0:T(8,128)(2,1)} async-done(((bf16[16,128,768]{2,1,0:T(8,128)(2,1)}), bf16[16,128,768]{2,1,0:T(8,128)(2,1)}, u32[]{:S(2)}, u32[]{:S(2)}) %all-to-all-start) | async-done | bytes 3145760 | tf_op jit(solution)/shard_map/all_to_all | solution.py:206
  100.0 6.8 gather_fusion.1
  107.5 6.2 slice.224
  113.8 9.7 reshape.1647
  124.2 11.8 convolution_bitcast_fusion.1
  141.5 9.5 fusion.126
  156.0 8.1 reshape.1649
  164.1 6.6 copy.237
  178.9 254.5 %while.45 = (s32[]{:T(128)}, f32[1,24,64,128]{3,2,1,0:T(8,128)S(1)}, f32[1]{0:T(128)}, f32[4,1,256,24,64]{2,0,4,3,1:T(4,128)}, f32[4,1,24,64,128]{4,3,2,1,0:T(8,...) while((s32[]{:T(128)}, ...), condition=%wide.region_4.6_spmd.clone, body=%wide.region_1.5_spmd.clone.sunk | while | flops 2526444544 | bytes 20096584 | solution.py:116
  183.2 9.3 fusion.244
  198.4 34.7 %dynamic_update_slice.74 = f32[4,1,256,24,64]{2,0,4,3,1:T(4,128)} dynamic-update-slice(f32[4,1,256,24,64]{2,0,4,3,1:T(4,128)} %get-tuple-element.1165, f32[1,1,256,24,64]{2,0,4,3,1:T(1,128)} %copy.373, s32[]{:T(128)} %get-tuple-element.1162, s32[]{:T(128)} %constant.237.clone.1..sunk, s32[]{:T(128)} %constant.237.clone.1..sunk, s32[]{:T(128)} %constant.237.clone.1..sunk, s32[]{:T(128)} %constant.237.clone.1..sunk) | dynamic-update-slice | bytes 3145732 | tf_op jit(solution)/shard_map/jvp()/while/body/jit(dynamic_update_index_in_dim)/dynamic_update_slice | solution.py:116
  246.7 9.3 fusion.244
  261.9 34.7 %dynamic_update_slice.74 = f32[4,1,256,24,64]{2,0,4,3,1:T(4,128)} dynamic-update-slice(f32[4,1,256,24,64]{2,0,4,3,1:T(4,128)} %get-tuple-element.1165, f32[1,1,256,24,64]{2,0,4,3,1:T(1,128)} %copy.373, s32[]{:T(128)} %get-tuple-element.1162, s32[]{:T(128)} %constant.237.clone.1..sunk, s32[]{:T(128)} %constant.237.clone.1..sunk, s32[]{:T(128)} %constant.237.clone.1..sunk, s32[]{:T(128)} %constant.237.clone.1..sunk) | dynamic-update-slice | bytes 3145732 | tf_op jit(solution)/shard_map/jvp()/while/body/jit(dynamic_update_index_in_dim)/dynamic_update_slice | solution.py:116
  310.4 9.3 fusion.244
  325.6 34.7 %dynamic_update_slice.74 = f32[4,1,256,24,64]{2,0,4,3,1:T(4,128)} dynamic-update-slice(f32[4,1,256,24,64]{2,0,4,3,1:T(4,128)} %get-tuple-element.1165, f32[1,1,256,24,64]{2,0,4,3,1:T(1,128)} %copy.373, s32[]{:T(128)} %get-tuple-element.1162, s32[]{:T(128)} %constant.237.clone.1..sunk, s32[]{:T(128)} %constant.237.clone.1..sunk, s32[]{:T(128)} %constant.237.clone.1..sunk, s32[]{:T(128)} %constant.237.clone.1..sunk) | dynamic-update-slice | bytes 3145732 | tf_op jit(solution)/shard_map/jvp()/while/body/jit(dynamic_update_index_in_dim)/dynamic_update_slice | solution.py:116
  374.0 9.3 fusion.244
  389.1 34.7 %dynamic_update_slice.74 = f32[4,1,256,24,64]{2,0,4,3,1:T(4,128)} dynamic-update-slice(f32[4,1,256,24,64]{2,0,4,3,1:T(4,128)} %get-tuple-element.1165, f32[1,1,256,24,64]{2,0,4,3,1:T(1,128)} %copy.373, s32[]{:T(128)} %get-tuple-element.1162, s32[]{:T(128)} %constant.237.clone.1..sunk, s32[]{:T(128)} %constant.237.clone.1..sunk, s32[]{:T(128)} %constant.237.clone.1..sunk, s32[]{:T(128)} %constant.237.clone.1..sunk) | dynamic-update-slice | bytes 3145732 | tf_op jit(solution)/shard_map/jvp()/while/body/jit(dynamic_update_index_in_dim)/dynamic_update_slice | solution.py:116
  433.4 8.3 transpose.177
  441.9 10.5 multiply_reduce_fusion.8
  458.8 7.9 fusion.131
  466.7 16.1 multiply_reduce_fusion.7
  482.9 8.1 reshape.1657
  497.6 514.2 %while.46 = (s32[]{:T(128)}, f32[24]{0:T(128)}, f32[1,24,64,128]{3,2,1,0:T(8,128)}, f32[4,1,256,24,64]{2,0,4,3,1:T(4,128)}, f32[4,1,256,24]{3,2,1,0:T(8,128)}, /...) while((s32[]{:T(128)}, f32[24]{0:T(128)}, ...), condition=%wide.region_21.24_spmd.clone, body=%wide.region_8.23_spmd.clone.sunk | while | flops 5772160000 | bytes 61074916 | solution.py:116
  498.5 4.4 constant_dynamic-slice_fusion.11
  533.2 11.8 fusion.264
  577.7 7.2 fusion.270
  587.7 34.7 %dynamic_update_slice.78 = f32[4,1,256,24,64]{2,0,4,3,1:T(4,128)} dynamic-update-slice(f32[4,1,256,24,64]{2,0,4,3,1:T(4,128)} %get-tuple-element.1215, f32[1,1,256,24,64]{2,0,4,3,1:T(1,128)} %copy.392, s32[]{:T(128)S(6)} %sub.331, s32[]{:T(128)} %constant.237.clone.1..sunk.1, s32[]{:T(128)} %constant.237.clone.1..sunk.1, s32[]{:T(128)} %constant.237.clone.1..sunk.1, s32[]{:T(128)} %constant.237.clone.1..sunk.1) | dynamic-update-slice | bytes 3145732 | tf_op jit(solution)/shard_map/transpose(jvp())/while/body/jit(dynamic_update_index_in_dim)/dynamic_update_slice | solution.py:116
  661.8 11.8 fusion.264
  706.3 7.2 fusion.270
  716.4 34.7 %dynamic_update_slice.78 = f32[4,1,256,24,64]{2,0,4,3,1:T(4,128)} dynamic-update-slice(f32[4,1,256,24,64]{2,0,4,3,1:T(4,128)} %get-tuple-element.1215, f32[1,1,256,24,64]{2,0,4,3,1:T(1,128)} %copy.392, s32[]{:T(128)S(6)} %sub.331, s32[]{:T(128)} %constant.237.clone.1..sunk.1, s32[]{:T(128)} %constant.237.clone.1..sunk.1, s32[]{:T(128)} %constant.237.clone.1..sunk.1, s32[]{:T(128)} %constant.237.clone.1..sunk.1) | dynamic-update-slice | bytes 3145732 | tf_op jit(solution)/shard_map/transpose(jvp())/while/body/jit(dynamic_update_index_in_dim)/dynamic_update_slice | solution.py:116
  754.8 4.4 constant_dynamic-slice_fusion.11
  790.6 11.8 fusion.264
  835.1 7.2 fusion.270
  845.2 34.7 %dynamic_update_slice.78 = f32[4,1,256,24,64]{2,0,4,3,1:T(4,128)} dynamic-update-slice(f32[4,1,256,24,64]{2,0,4,3,1:T(4,128)} %get-tuple-element.1215, f32[1,1,256,24,64]{2,0,4,3,1:T(1,128)} %copy.392, s32[]{:T(128)S(6)} %sub.331, s32[]{:T(128)} %constant.237.clone.1..sunk.1, s32[]{:T(128)} %constant.237.clone.1..sunk.1, s32[]{:T(128)} %constant.237.clone.1..sunk.1, s32[]{:T(128)} %constant.237.clone.1..sunk.1) | dynamic-update-slice | bytes 3145732 | tf_op jit(solution)/shard_map/transpose(jvp())/while/body/jit(dynamic_update_index_in_dim)/dynamic_update_slice | solution.py:116
  919.2 11.8 fusion.264
  963.8 7.2 fusion.270
  973.8 34.7 %dynamic_update_slice.78 = f32[4,1,256,24,64]{2,0,4,3,1:T(4,128)} dynamic-update-slice(f32[4,1,256,24,64]{2,0,4,3,1:T(4,128)} %get-tuple-element.1215, f32[1,1,256,24,64]{2,0,4,3,1:T(1,128)} %copy.392, s32[]{:T(128)S(6)} %sub.331, s32[]{:T(128)} %constant.237.clone.1..sunk.1, s32[]{:T(128)} %constant.237.clone.1..sunk.1, s32[]{:T(128)} %constant.237.clone.1..sunk.1, s32[]{:T(128)} %constant.237.clone.1..sunk.1) | dynamic-update-slice | bytes 3145732 | tf_op jit(solution)/shard_map/transpose(jvp())/while/body/jit(dynamic_update_index_in_dim)/dynamic_update_slice | solution.py:116
  1011.8 8.3 transpose.181
  1020.1 8.0 multiply_add_fusion.1
  1028.7 19.7 %multiply_reduce_fusion.5 = (f32[1792]{0:T(1024)S(1)}, f32[1792]{0:T(1024)S(1)}, f32[1792]{0:T(1024)S(1)}, f32[1792]{0:T(1024)S(1)}, f32[1792]{0:T(1024)S(1)}, /*index=5*/f32[1,1024,1792]{1,2,0:T(8,128)S(1)}) fusion(f32[1,1024,1792]{1,2,0:T(8,128)} %copy-done.6, f32[1024]{0:T(1024)S(1)} %bitcast.707, f32[1024]{0:T(1024)S(1)} %bitcast.701, ...), kind=kLoop, calls=%fused_computation.202 | loop fusion | flops 44031232 | bytes 36752384 | tf_op jit(solution)/shard_map/transpose(jvp())/reduce_sum | solution.py:71
  1048.5 10.5 multiply_multiply_fusion.4
  1060.3 15.0 pad_add_fusion
  1075.3 14.6 fusion.150
  1090.0 12.5 fusion.138
  1102.5 7.6 fusion.145
  1110.2 11.1 reshape.1661
  1121.4 5.7 reshape.1663
  1128.4 87.9 %dynamic-update-slice.1 = f32[3768320]{0:T(1024)} dynamic-update-slice(f32[3768320]{0:T(1024)} %constant_dynamic-update-slice_fusion.6, f32[2574336]{0:T(1024)} %reshape.1661, s32[]{} %constant.327) | dynamic-update-slice | bytes 20594692
  1224.9 41.0 %dynamic-update-slice.8 = f32[3768320]{0:T(1024)} dynamic-update-slice(f32[3768320]{0:T(1024)} %constant_dynamic-update-slice_fusion, f32[1179648]{0:T(1024)} %reshape.1663, s32[]{} %constant.334) | dynamic-update-slice | bytes 9437188
  1269.1 258.3 %all-reduce.26.cloned.1.call-done = f32[3768320]{0:T(1024)} async-done(((f32[3768320]{0:T(1024)}), f32[3768320]{0:T(1024)}) %all-reduce.26.cloned.1.call-update) | async-done | bytes 15073296
  1533.0 145.1 %all-reduce.24.cloned.1.call-done = f32[942080]{0:T(1024)} async-done(((f32[942080]{0:T(1024)}), f32[942080]{0:T(1024)}) %all-reduce.24.cloned.1.call-update) | async-done | bytes 3768336 | tf_op jit(solution)/shard_map/psum | solution.py:290
  1678.1 11.5 multiply_subtract_fusion
  1689.9 5.9 fusion.174
  1695.8 9.4 gather_fusion.3
  1709.0 9.4 gather_fusion.5
  1718.5 5.3 broadcast_select_fusion.2
  1726.7 4.9 copy.241
  1731.6 4.7 all-to-all-start.1
  1736.3 4.9 copy.255
  1741.2 66.2 %all-to-all-done.1 = bf16[2,1024,768]{2,0,1:T(2,128)(2,1)} async-done(((bf16[2,1024,768]{2,0,1:T(2,128)(2,1)}), bf16[2,1024,768]{2,0,1:T(2,128)(2,1)}, u32[]{:S(2)}, u32[]{:S(2)}) %all-to-all-start.1) | async-done | bytes 3145760 | tf_op jit(solution)/shard_map/all_to_all | solution.py:268
  1816.1 65.8 %all-to-all-done.2 = bf16[2,1024,768]{2,0,1:T(2,128)(2,1)S(1)} async-done(((bf16[2,1024,768]{2,0,1:T(2,128)(2,1)}), bf16[2,1024,768]{2,0,1:T(2,128)(2,1)S(1)}, u32[]{:S(2)}, u32[]{:S(2)}) %all-to-all-start.2) | async-done | bytes 3145760 | tf_op jit(solution)/shard_map/all_to_all | solution.py:269
  1892.2 5.2 broadcast_select_fusion.4
  1897.5 11.7 copy.460
  (673 shorter events, 454.0 us)
Async XLA Ops:
  7.2 100.3 %all-gather.3.cloned.1.call-start = ((), (), s32[]{:S(2)}) async-start(), calls=%async_computation.3 | async-start | bytes 9420800 | tf_op jit(solution)/shard_map/all_gather | solution.py:184
  18.1 78.1 %all-to-all-start = ((bf16[16,128,768]{2,1,0:T(8,128)(2,1)}), bf16[16,128,768]{2,1,0:T(8,128)(2,1)}, u32[]{:S(2)}, u32[]{:S(2)}) async-start(bf16[16,128,768]{2,1,0:T(8,128)(2,1)} %broadcast_select_fusion.6), calls=%async_computation | async-start | bytes 6291456 | tf_op jit(solution)/shard_map/all_to_all | solution.py:206
  25.4 1502.0 %all-reduce.26.cloned.1.call-start = ((), (), s32[]{:S(2)}) async-start(), calls=%async_computation.6 | async-start | bytes 30146560
  27.1 97.1 %copy-start.60 = (pred[1024]{0:T(1024)(128)(4,1)}, pred[1024]{0:T(1024)(128)(4,1)S(1)}, u32[]{:S(2)}) copy-start(pred[1024]{0:T(1024)(128)(4,1)S(1)} %get-tuple-element.907) | copy-start | bytes 3076
  27.1 114.4 %copy-start.33 = (f32[1024]{0:T(1024)}, f32[1024]{0:T(1024)S(1)}, u32[]{:S(2)}) copy-start(f32[1024]{0:T(1024)S(1)} %get-tuple-element.908) | copy-start | bytes 12292
  27.2 114.3 %copy-start.35 = (f32[1,1024]{1,0:T(1,128)}, f32[1,1024]{1,0:T(1,128)S(1)}, u32[]{:S(2)}) copy-start(f32[1,1024]{1,0:T(1,128)S(1)} %get-tuple-element.896) | copy-start | bytes 12292
  27.2 114.3 %copy-start.37 = (f32[1,1024]{1,0:T(1,128)}, f32[1,1024]{1,0:T(1,128)S(1)}, u32[]{:S(2)}) copy-start(f32[1,1024]{1,0:T(1,128)S(1)} %get-tuple-element.897) | copy-start | bytes 12292
  27.2 114.3 %copy-start.39 = (f32[1,1024]{1,0:T(1,128)}, f32[1,1024]{1,0:T(1,128)S(1)}, u32[]{:S(2)}) copy-start(f32[1,1024]{1,0:T(1,128)S(1)} %get-tuple-element.898) | copy-start | bytes 12292
  106.8 17.4 copy-start.9
  107.5 16.0 copy-start.43
  107.5 16.7 copy-start.50
  124.2 11.8 copy-start.52
  441.9 24.8 %copy-start.23 = (f32[1536]{0:T(1024)}, f32[1536]{0:T(1024)S(1)}, u32[]{:S(2)}) copy-start(f32[1536]{0:T(1024)S(1)} %mul.958) | copy-start | bytes 18436
  452.4 14.3 copy-start.54
  497.7 14.7 copy-start.41
  533.1 11.8 copy-start.7
  533.1 11.8 copy-start.11
  533.1 13.8 copy-start.3
  577.7 44.8 %copy-start.18 = (f32[256,24]{0,1:T(8,128)S(1)}, f32[256,24]{0,1:T(8,128)}, u32[]{:S(2)}) copy-start(f32[256,24]{0,1:T(8,128)} %copy.390) | copy-start | bytes 73732 | tf_op jit(solution)/shard_map/transpose(jvp())/while
  584.8 39.9 %copy-start.57 = (f32[24]{0:T(128)S(1)}, f32[24]{0:T(128)}, u32[]{:S(2)}) copy-start(f32[24]{0:T(128)} %get-tuple-element.1213) | copy-start | bytes 292 | tf_op jit(solution)/shard_map/transpose(jvp())/while
  584.8 40.4 %copy-start.16 = (f32[4,1,256,128]{3,2,1,0:T(8,128)S(1)}, f32[4,1,256,128]{3,2,1,0:T(8,128)}, u32[]{:S(2)}) copy-start(f32[4,1,256,128]{3,2,1,0:T(8,128)} %copy-done.15) | copy-start | bytes 1572868 | tf_op jit(solution)/shard_map/transpose(jvp())/while
  584.9 40.4 %copy-start.42 = (f32[24]{0:T(128)S(1)}, f32[24]{0:T(128)}, u32[]{:S(2)}) copy-start(f32[24]{0:T(128)} %copy-done.41) | copy-start | bytes 292 | tf_op jit(solution)/shard_map/transpose(jvp())/while
  625.3 15.9 copy-start.41
  661.8 13.8 copy-start.3
  706.3 44.8 %copy-start.18 = (f32[256,24]{0,1:T(8,128)S(1)}, f32[256,24]{0,1:T(8,128)}, u32[]{:S(2)}) copy-start(f32[256,24]{0,1:T(8,128)} %copy.390) | copy-start | bytes 73732 | tf_op jit(solution)/shard_map/transpose(jvp())/while
  713.5 39.9 %copy-start.57 = (f32[24]{0:T(128)S(1)}, f32[24]{0:T(128)}, u32[]{:S(2)}) copy-start(f32[24]{0:T(128)} %get-tuple-element.1213) | copy-start | bytes 292 | tf_op jit(solution)/shard_map/transpose(jvp())/while
  713.5 40.4 %copy-start.16 = (f32[4,1,256,128]{3,2,1,0:T(8,128)S(1)}, f32[4,1,256,128]{3,2,1,0:T(8,128)}, u32[]{:S(2)}) copy-start(f32[4,1,256,128]{3,2,1,0:T(8,128)} %copy-done.15) | copy-start | bytes 1572868 | tf_op jit(solution)/shard_map/transpose(jvp())/while
  713.6 40.4 %copy-start.42 = (f32[24]{0:T(128)S(1)}, f32[24]{0:T(128)}, u32[]{:S(2)}) copy-start(f32[24]{0:T(128)} %copy-done.41) | copy-start | bytes 292 | tf_op jit(solution)/shard_map/transpose(jvp())/while
  754.0 15.9 copy-start.41
  790.6 11.8 copy-start.7
  790.6 11.8 copy-start.11
  790.6 13.8 copy-start.3
  835.1 44.8 %copy-start.18 = (f32[256,24]{0,1:T(8,128)S(1)}, f32[256,24]{0,1:T(8,128)}, u32[]{:S(2)}) copy-start(f32[256,24]{0,1:T(8,128)} %copy.390) | copy-start | bytes 73732 | tf_op jit(solution)/shard_map/transpose(jvp())/while
  842.3 39.9 %copy-start.57 = (f32[24]{0:T(128)S(1)}, f32[24]{0:T(128)}, u32[]{:S(2)}) copy-start(f32[24]{0:T(128)} %get-tuple-element.1213) | copy-start | bytes 292 | tf_op jit(solution)/shard_map/transpose(jvp())/while
  842.3 40.4 %copy-start.16 = (f32[4,1,256,128]{3,2,1,0:T(8,128)S(1)}, f32[4,1,256,128]{3,2,1,0:T(8,128)}, u32[]{:S(2)}) copy-start(f32[4,1,256,128]{3,2,1,0:T(8,128)} %copy-done.15) | copy-start | bytes 1572868 | tf_op jit(solution)/shard_map/transpose(jvp())/while
  842.3 40.4 %copy-start.42 = (f32[24]{0:T(128)S(1)}, f32[24]{0:T(128)}, u32[]{:S(2)}) copy-start(f32[24]{0:T(128)} %copy-done.41) | copy-start | bytes 292 | tf_op jit(solution)/shard_map/transpose(jvp())/while
  882.7 15.8 copy-start.41
  919.2 11.8 copy-start.7
  919.2 11.8 copy-start.11
  919.2 13.8 copy-start.3
  963.8 44.8 %copy-start.18 = (f32[256,24]{0,1:T(8,128)S(1)}, f32[256,24]{0,1:T(8,128)}, u32[]{:S(2)}) copy-start(f32[256,24]{0,1:T(8,128)} %copy.390) | copy-start | bytes 73732 | tf_op jit(solution)/shard_map/transpose(jvp())/while
  970.9 39.9 %copy-start.57 = (f32[24]{0:T(128)S(1)}, f32[24]{0:T(128)}, u32[]{:S(2)}) copy-start(f32[24]{0:T(128)} %get-tuple-element.1213) | copy-start | bytes 292 | tf_op jit(solution)/shard_map/transpose(jvp())/while
  971.0 40.4 %copy-start.16 = (f32[4,1,256,128]{3,2,1,0:T(8,128)S(1)}, f32[4,1,256,128]{3,2,1,0:T(8,128)}, u32[]{:S(2)}) copy-start(f32[4,1,256,128]{3,2,1,0:T(8,128)} %copy-done.15) | copy-start | bytes 1572868 | tf_op jit(solution)/shard_map/transpose(jvp())/while
  971.0 40.4 %copy-start.42 = (f32[24]{0:T(128)S(1)}, f32[24]{0:T(128)}, u32[]{:S(2)}) copy-start(f32[24]{0:T(128)} %copy-done.41) | copy-start | bytes 292 | tf_op jit(solution)/shard_map/transpose(jvp())/while
  1028.7 19.7 %copy-start.26 = (f32[1792]{0:T(1024)S(1)}, f32[1792]{0:T(1024)}, u32[]{:S(2)}) copy-start(f32[1792]{0:T(1024)} %copy-done.25) | copy-start | bytes 21508
  1028.7 19.7 %copy-start.28 = (f32[1792]{0:T(1024)S(1)}, f32[1792]{0:T(1024)}, u32[]{:S(2)}) copy-start(f32[1792]{0:T(1024)} %copy-done.27) | copy-start | bytes 21508
  1028.7 19.7 %copy-start.30 = (f32[1792]{0:T(1024)S(1)}, f32[1792]{0:T(1024)}, u32[]{:S(2)}) copy-start(f32[1792]{0:T(1024)} %copy-done.29) | copy-start | bytes 21508
  1028.7 19.7 %copy-start.32 = (f32[1792]{0:T(1024)S(1)}, f32[1792]{0:T(1024)}, u32[]{:S(2)}) copy-start(f32[1792]{0:T(1024)} %copy-done.31) | copy-start | bytes 21508
  1060.3 15.0 copy-start.10
  1060.3 15.0 copy-start.51
  1060.3 15.0 copy-start.53
  1060.3 15.0 copy-start.61
  1090.0 12.5 copy-start.22
  1090.0 12.5 copy-start.46
  1090.0 12.5 copy-start.55
  1128.4 91.9 %copy-start.59 = (f32[24]{0:T(128)S(1)}, f32[24]{0:T(128)}, u32[]{:S(2)}) copy-start(f32[24]{0:T(128)} %get-tuple-element.474) | copy-start | bytes 292
  1128.4 95.2 %copy-start.62 = (f32[1536]{0:T(1024)S(1)}, f32[1536]{0:T(1024)}, u32[]{:S(2)}) copy-start(f32[1536]{0:T(1024)} %get-tuple-element.783) | copy-start | bytes 18436
  1267.2 265.1 %copy-start.65 = (f32[2]{0:T(128)S(1)}, f32[2]{0:T(128)}, u32[]{:S(2)}) copy-start(f32[2]{0:T(128)} %param.24) | copy-start | bytes 28
  1267.3 410.9 %all-reduce.24.cloned.1.call-start = ((), (), s32[]{:S(2)}) async-start(), calls=%async_computation.4 | async-start | bytes 7536640 | tf_op jit(solution)/shard_map/psum | solution.py:290
  1531.6 365.9 %all-gather.5.cloned.1.call-start = ((), (), s32[]{:S(2)}) async-start(), calls=%async_computation.5 | async-start | bytes 18841600 | tf_op jit(solution)/shard_map/all_gather | solution.py:294
  1731.6 75.9 %all-to-all-start.1 = ((bf16[2,1024,768]{2,0,1:T(2,128)(2,1)}), bf16[2,1024,768]{2,0,1:T(2,128)(2,1)}, u32[]{:S(2)}, u32[]{:S(2)}) async-start(bf16[2,1024,768]{2,0,1:T(2,128)(2,1)} %copy.241), calls=%async_computation.1 | async-start | bytes 6291456 | tf_op jit(solution)/shard_map/all_to_all | solution.py:268
  1736.3 74.8 %copy-start.56 = (s32[8,2]{1,0:T(8,128)S(1)}, s32[8,2]{1,0:T(8,128)}, u32[]{:S(2)}) copy-start(s32[8,2]{1,0:T(8,128)} %get-tuple-element.789) | copy-start | bytes 196
  1807.4 74.5 %all-to-all-start.2 = ((bf16[2,1024,768]{2,0,1:T(2,128)(2,1)}), bf16[2,1024,768]{2,0,1:T(2,128)(2,1)S(1)}, u32[]{:S(2)}, u32[]{:S(2)}) async-start(bf16[2,1024,768]{2,0,1:T(2,128)(2,1)} %copy.255), calls=%async_computation.2 | async-start | bytes 6291456 | tf_op jit(solution)/shard_map/all_to_all | solution.py:269
  1897.5 13.8 copy-start.1
  (44 other events, 272.2 us)
Sparse Core Ops, SparseCore 0:
  11.0 56.1 all-gather.2
  1267.4 259.9 all-reduce.25
  1532.1 145.9 all-reduce.23
  1689.8 95.2 all-gather.4
where the time goes:
time: 1950 us; the launch traced here: 1920 us
  local copies, waits for them, and re-layouts  772 us (40%)
  waiting for transfers between devices  604 us (31%)
  matrix products  276 us (14%)
  other arithmetic  221 us (11%)
    dynamic_update_slice x28, local copies, waits for them, and re-layouts, span_scan(): lax.scan(jax.checkpoint(advance), initial, (split_blocks(x_heads), split_...  324 us
    unnamed x5, waiting for transfers between devices  258 us
    unnamed x130, local copies, waits for them, and re-layouts  167 us
    psum x1, waiting for transfers between devices, on_device(): grad_shard = lax.psum(grad_shard, 'dp')  145 us
    dot_general x12, matrix products, advance(): jnp.einsum('shtr,srhp->sthp', mixing, x_blk, precision=EXACT_MATMUL)  113 us
    all_to_all x1, waiting for transfers between devices, on_device(): lax.all_to_all(dealt_rows, 'dp', split_axis=0, concat_axis=1, tiled=True)  68.9 us
    all_to_all x1, waiting for transfers between devices, on_device(): lax.all_to_all(result, 'dp', split_axis=1, concat_axis=0, tiled=True)  66.2 us
    all_to_all x1, waiting for transfers between devices, on_device(): lax.all_to_all(grad_input, 'dp', split_axis=1, concat_axis=0, tiled=True)  65.8 us
  transfers between devices with their start and end apart: 7, of which 5 were waited for; matrix products, arithmetic and copies ran while one was open for 5% of the time, Pallas kernels for 0%

commit v1 on v0

--- a/solution.py
+++ b/solution.py
@@ -287,7 +287,7 @@
     used_len = sum((piece.shape[0] for piece in laid))
     flat_grad = jnp.concatenate(laid + [jnp.zeros((vector_len - used_len,), jnp.float32)])
     grad_shard = lax.psum_scatter(flat_grad, "zero", scatter_dimension=0, tiled=True)
-    grad_shard = lax.psum(grad_shard, "dp")
+    grad_shard = jnp.sum(lax.all_gather(grad_shard, "dp"), axis=0)
     new_shard, first_next, second_next = adam_update(
         master, moment_one, moment_two, grad_shard, adam_rates, iteration_tally
     )

time: 1950 us -> 2450 us (1.26)
  waiting for transfers between devices: 604 us -> 1030 us
  other arithmetic: 221 us -> 264 us
    all_gather x0 -> x1, waiting for transfers between devices: none -> 573 us  [on_device(): grad_shard = jnp.sum(lax.all_gather(grad_shard, 'dp'), axis=0)]
    psum x1 -> x0, waiting for transfers between devices: 145 us -> none  [on_device(): grad_shard = lax.psum(grad_shard, 'dp')]
    reduce_sum x0 -> x1, other arithmetic: none -> 42.8 us  [on_device(): grad_shard = jnp.sum(lax.all_gather(grad_shard, 'dp'), axis=0)]
    all_gather x0 -> x1, local copies, waits for them, and re-layouts: none -> 26.6 us  [on_device(): grad_shard = jnp.sum(lax.all_gather(grad_shard, 'dp'), axis=0)]
    unnamed x130 -> x127, local copies, waits for them, and re-layouts: 167 us -> 164 us
  transfers between devices with their start and end apart: 7 -> 7, of which waited for: 5 -> 5; matrix products, arithmetic and copies ran while one was open for 5% -> 4% of each run, Pallas kernels for 0% -> 0%
where the time goes in v1:
time: 2450 us; the launch traced here: 2410 us
  waiting for transfers between devices  1030 us (42%)
  local copies, waits for them, and re-layouts  795 us (32%)
  matrix products  276 us (11%)
  other arithmetic  264 us (11%)
    all_gather x1, waiting for transfers between devices, on_device(): grad_shard = jnp.sum(lax.all_gather(grad_shard, 'dp'), axis=0)  573 us
    dynamic_update_slice x28, local copies, waits for them, and re-layouts, span_scan(): lax.scan(jax.checkpoint(advance), initial, (split_blocks(x_heads), split_...  324 us
    unnamed x5, waiting for transfers between devices  258 us
    unnamed x127, local copies, waits for them, and re-layouts  164 us
    dot_general x12, matrix products, advance(): jnp.einsum('shtr,srhp->sthp', mixing, x_blk, precision=EXACT_MATMUL)  113 us
    all_to_all x1, waiting for transfers between devices, on_device(): lax.all_to_all(dealt_rows, 'dp', split_axis=0, concat_axis=1, tiled=True)  68.9 us
    all_to_all x1, waiting for transfers between devices, on_device(): lax.all_to_all(result, 'dp', split_axis=1, concat_axis=0, tiled=True)  66.2 us
    all_to_all x1, waiting for transfers between devices, on_device(): lax.all_to_all(grad_input, 'dp', split_axis=1, concat_axis=0, tiled=True)  65.9 us
  transfers between devices with their start and end apart: 7, of which 5 were waited for; matrix products, arithmetic and copies ran while one was open for 4% of the time, Pallas kernels for 0%

profile of v1, /device:TPU:0, one launch (start us, length us, event | category | flops | bytes accessed | tf_op | source)
XLA Modules:
  0.0 2412.4 jit_solution(2115502807775639696)
XLA Ops:
  18.1 7.3 all-to-all-start
  27.3 68.9 %all-to-all-done = bf16[16,128,768]{2,1,0:T(8,128)(2,1)} async-done(((bf16[16,128,768]{2,1,0:T(8,128)(2,1)}), bf16[16,128,768]{2,1,0:T(8,128)(2,1)}, u32[]{:S(2)}, u32[]{:S(2)}) %all-to-all-start) | async-done | bytes 3145760 | tf_op jit(solution)/shard_map/all_to_all | solution.py:206
  100.0 6.8 gather_fusion.1
  107.5 6.2 slice.224
  113.7 9.7 reshape.1647
  124.2 11.7 convolution_bitcast_fusion.1
  141.4 9.6 fusion.126
  156.0 8.1 reshape.1649
  164.1 6.6 copy.237
  179.0 255.2 %while.45 = (s32[]{:T(128)}, f32[1,24,64,128]{3,2,1,0:T(8,128)S(1)}, f32[1]{0:T(128)}, f32[4,1,256,24,64]{2,0,4,3,1:T(4,128)}, f32[4,1,24,64,128]{4,3,2,1,0:T(8,...) while((s32[]{:T(128)}, ...), condition=%wide.region_4.6_spmd.clone, body=%wide.region_1.5_spmd.clone.sunk | while | flops 2526444544 | bytes 20096584 | solution.py:116
  183.6 9.3 fusion.244
  198.8 34.7 %dynamic_update_slice.74 = f32[4,1,256,24,64]{2,0,4,3,1:T(4,128)} dynamic-update-slice(f32[4,1,256,24,64]{2,0,4,3,1:T(4,128)} %get-tuple-element.1165, f32[1,1,256,24,64]{2,0,4,3,1:T(1,128)} %copy.374, s32[]{:T(128)} %get-tuple-element.1162, s32[]{:T(128)} %constant.237.clone.1..sunk, s32[]{:T(128)} %constant.237.clone.1..sunk, s32[]{:T(128)} %constant.237.clone.1..sunk, s32[]{:T(128)} %constant.237.clone.1..sunk) | dynamic-update-slice | bytes 3145732 | tf_op jit(solution)/shard_map/jvp()/while/body/jit(dynamic_update_index_in_dim)/dynamic_update_slice | solution.py:116
  247.3 9.3 fusion.244
  262.5 34.7 %dynamic_update_slice.74 = f32[4,1,256,24,64]{2,0,4,3,1:T(4,128)} dynamic-update-slice(f32[4,1,256,24,64]{2,0,4,3,1:T(4,128)} %get-tuple-element.1165, f32[1,1,256,24,64]{2,0,4,3,1:T(1,128)} %copy.374, s32[]{:T(128)} %get-tuple-element.1162, s32[]{:T(128)} %constant.237.clone.1..sunk, s32[]{:T(128)} %constant.237.clone.1..sunk, s32[]{:T(128)} %constant.237.clone.1..sunk, s32[]{:T(128)} %constant.237.clone.1..sunk) | dynamic-update-slice | bytes 3145732 | tf_op jit(solution)/shard_map/jvp()/while/body/jit(dynamic_update_index_in_dim)/dynamic_update_slice | solution.py:116
  311.1 9.3 fusion.244
  326.3 34.7 %dynamic_update_slice.74 = f32[4,1,256,24,64]{2,0,4,3,1:T(4,128)} dynamic-update-slice(f32[4,1,256,24,64]{2,0,4,3,1:T(4,128)} %get-tuple-element.1165, f32[1,1,256,24,64]{2,0,4,3,1:T(1,128)} %copy.374, s32[]{:T(128)} %get-tuple-element.1162, s32[]{:T(128)} %constant.237.clone.1..sunk, s32[]{:T(128)} %constant.237.clone.1..sunk, s32[]{:T(128)} %constant.237.clone.1..sunk, s32[]{:T(128)} %constant.237.clone.1..sunk) | dynamic-update-slice | bytes 3145732 | tf_op jit(solution)/shard_map/jvp()/while/body/jit(dynamic_update_index_in_dim)/dynamic_update_slice | solution.py:116
  374.7 9.3 fusion.244
  389.9 34.7 %dynamic_update_slice.74 = f32[4,1,256,24,64]{2,0,4,3,1:T(4,128)} dynamic-update-slice(f32[4,1,256,24,64]{2,0,4,3,1:T(4,128)} %get-tuple-element.1165, f32[1,1,256,24,64]{2,0,4,3,1:T(1,128)} %copy.374, s32[]{:T(128)} %get-tuple-element.1162, s32[]{:T(128)} %constant.237.clone.1..sunk, s32[]{:T(128)} %constant.237.clone.1..sunk, s32[]{:T(128)} %constant.237.clone.1..sunk, s32[]{:T(128)} %constant.237.clone.1..sunk) | dynamic-update-slice | bytes 3145732 | tf_op jit(solution)/shard_map/jvp()/while/body/jit(dynamic_update_index_in_dim)/dynamic_update_slice | solution.py:116
  434.3 8.3 transpose.177
  442.7 10.4 multiply_reduce_fusion.8
  459.2 7.9 fusion.131
  467.2 16.1 multiply_reduce_fusion.7
  483.2 8.1 reshape.1657
  497.9 513.7 %while.46 = (s32[]{:T(128)}, f32[24]{0:T(128)}, f32[1,24,64,128]{3,2,1,0:T(8,128)}, f32[4,1,256,24,64]{2,0,4,3,1:T(4,128)}, f32[4,1,256,24]{3,2,1,0:T(8,128)}, /...) while((s32[]{:T(128)}, f32[24]{0:T(128)}, ...), condition=%wide.region_21.24_spmd.clone, body=%wide.region_8.23_spmd.clone.sunk | while | flops 5772160000 | bytes 61074916 | solution.py:116
  533.5 11.8 fusion.264
  578.0 7.2 fusion.270
  588.1 34.7 %dynamic_update_slice.78 = f32[4,1,256,24,64]{2,0,4,3,1:T(4,128)} dynamic-update-slice(f32[4,1,256,24,64]{2,0,4,3,1:T(4,128)} %get-tuple-element.1215, f32[1,1,256,24,64]{2,0,4,3,1:T(1,128)} %copy.393, s32[]{:T(128)S(6)} %sub.331, s32[]{:T(128)} %constant.237.clone.1..sunk.1, s32[]{:T(128)} %constant.237.clone.1..sunk.1, s32[]{:T(128)} %constant.237.clone.1..sunk.1, s32[]{:T(128)} %constant.237.clone.1..sunk.1) | dynamic-update-slice | bytes 3145732 | tf_op jit(solution)/shard_map/transpose(jvp())/while/body/jit(dynamic_update_index_in_dim)/dynamic_update_slice | solution.py:116
  662.1 11.8 fusion.264
  706.5 7.2 fusion.270
  716.6 34.7 %dynamic_update_slice.78 = f32[4,1,256,24,64]{2,0,4,3,1:T(4,128)} dynamic-update-slice(f32[4,1,256,24,64]{2,0,4,3,1:T(4,128)} %get-tuple-element.1215, f32[1,1,256,24,64]{2,0,4,3,1:T(1,128)} %copy.393, s32[]{:T(128)S(6)} %sub.331, s32[]{:T(128)} %constant.237.clone.1..sunk.1, s32[]{:T(128)} %constant.237.clone.1..sunk.1, s32[]{:T(128)} %constant.237.clone.1..sunk.1, s32[]{:T(128)} %constant.237.clone.1..sunk.1) | dynamic-update-slice | bytes 3145732 | tf_op jit(solution)/shard_map/transpose(jvp())/while/body/jit(dynamic_update_index_in_dim)/dynamic_update_slice | solution.py:116
  790.7 11.8 fusion.264
  835.1 7.2 fusion.270
  845.2 34.7 %dynamic_update_slice.78 = f32[4,1,256,24,64]{2,0,4,3,1:T(4,128)} dynamic-update-slice(f32[4,1,256,24,64]{2,0,4,3,1:T(4,128)} %get-tuple-element.1215, f32[1,1,256,24,64]{2,0,4,3,1:T(1,128)} %copy.393, s32[]{:T(128)S(6)} %sub.331, s32[]{:T(128)} %constant.237.clone.1..sunk.1, s32[]{:T(128)} %constant.237.clone.1..sunk.1, s32[]{:T(128)} %constant.237.clone.1..sunk.1, s32[]{:T(128)} %constant.237.clone.1..sunk.1) | dynamic-update-slice | bytes 3145732 | tf_op jit(solution)/shard_map/transpose(jvp())/while/body/jit(dynamic_update_index_in_dim)/dynamic_update_slice | solution.py:116
  919.3 11.8 fusion.264
  963.8 7.2 fusion.270
  973.8 34.7 %dynamic_update_slice.78 = f32[4,1,256,24,64]{2,0,4,3,1:T(4,128)} dynamic-update-slice(f32[4,1,256,24,64]{2,0,4,3,1:T(4,128)} %get-tuple-element.1215, f32[1,1,256,24,64]{2,0,4,3,1:T(1,128)} %copy.393, s32[]{:T(128)S(6)} %sub.331, s32[]{:T(128)} %constant.237.clone.1..sunk.1, s32[]{:T(128)} %constant.237.clone.1..sunk.1, s32[]{:T(128)} %constant.237.clone.1..sunk.1, s32[]{:T(128)} %constant.237.clone.1..sunk.1) | dynamic-update-slice | bytes 3145732 | tf_op jit(solution)/shard_map/transpose(jvp())/while/body/jit(dynamic_update_index_in_dim)/dynamic_update_slice | solution.py:116
  1011.6 8.3 transpose.181
  1019.9 7.9 multiply_add_fusion.1
  1028.4 19.6 multiply_reduce_fusion.5
  1048.1 10.5 multiply_multiply_fusion.4
  1060.0 15.0 pad_add_fusion
  1075.1 14.5 fusion.150
  1089.6 12.5 fusion.138
  1102.2 7.7 fusion.145
  1110.0 11.1 reshape.1661
  1121.2 5.7 reshape.1663
  1128.2 87.9 %dynamic-update-slice.1 = f32[3768320]{0:T(1024)} dynamic-update-slice(f32[3768320]{0:T(1024)} %constant_dynamic-update-slice_fusion.6, f32[2574336]{0:T(1024)} %reshape.1661, s32[]{} %constant.327) | dynamic-update-slice | bytes 20594692
  1224.8 41.0 %dynamic-update-slice.8 = f32[3768320]{0:T(1024)} dynamic-update-slice(f32[3768320]{0:T(1024)} %constant_dynamic-update-slice_fusion, f32[1179648]{0:T(1024)} %reshape.1663, s32[]{} %constant.334) | dynamic-update-slice | bytes 9437188
  1268.9 258.3 %all-reduce.23.cloned.1.call-done = f32[3768320]{0:T(1024)} async-done(((f32[3768320]{0:T(1024)}), f32[3768320]{0:T(1024)}) %all-reduce.23.cloned.1.call-update) | async-done | bytes 15073296
  1532.8 572.8 %all-gather.9.cloned.1.call-done = f32[7536640]{0:T(1024)} async-done(((f32[942080]{0:T(1024)}), f32[7536640]{0:T(1024)}) %all-gather.9.cloned.1.call-update) | async-done | bytes 30146576 | tf_op jit(solution)/shard_map/all_gather | solution.py:290
  2105.7 26.6 %reshape.1737 = f32[8,942080]{1,0:T(8,128)} reshape(f32[7536640]{0:T(1024)} %all-gather.9.cloned.1.call-done) | data formatting | bytes 60293120 | tf_op jit(solution)/shard_map/all_gather | solution.py:290
  2132.2 42.8 %reduce_sum.247 = f32[942080]{0:T(1024)} reduce(f32[8,942080]{1,0:T(8,128)} %reshape.1737, f32[]{:T(128)} %constant.241.clone.1), dimensions={0}, to_apply=%region_34.37 | reduce | flops 6594560 | bytes 33914884 | tf_op jit(solution)/shard_map/reduce_sum | solution.py:290
  2175.0 11.6 multiply_subtract_fusion
  2186.8 5.9 fusion.174
  2192.8 9.5 gather_fusion.3
  2206.3 9.4 gather_fusion.5
  2215.7 5.3 broadcast_select_fusion.2
  2224.1 4.9 copy.241
  2229.0 4.8 all-to-all-start.1
  2233.8 4.9 copy.255
  2238.7 66.2 %all-to-all-done.1 = bf16[2,1024,768]{2,0,1:T(2,128)(2,1)} async-done(((bf16[2,1024,768]{2,0,1:T(2,128)(2,1)}), bf16[2,1024,768]{2,0,1:T(2,128)(2,1)}, u32[]{:S(2)}, u32[]{:S(2)}) %all-to-all-start.1) | async-done | bytes 3145760 | tf_op jit(solution)/shard_map/all_to_all | solution.py:268
  2313.5 65.9 %all-to-all-done.2 = bf16[2,1024,768]{2,0,1:T(2,128)(2,1)S(1)} async-done(((bf16[2,1024,768]{2,0,1:T(2,128)(2,1)}), bf16[2,1024,768]{2,0,1:T(2,128)(2,1)S(1)}, u32[]{:S(2)}, u32[]{:S(2)}) %all-to-all-start.2) | async-done | bytes 3145760 | tf_op jit(solution)/shard_map/all_to_all | solution.py:269
  2389.7 5.2 broadcast_select_fusion.4
  2394.9 10.8 copy.461
  (672 shorter events, 461.2 us)
Async XLA Ops:
  7.2 100.3 %all-gather.5.cloned.1.call-start = ((), (), s32[]{:S(2)}) async-start(), calls=%async_computation.3 | async-start | bytes 9420800 | tf_op jit(solution)/shard_map/all_gather | solution.py:184
  18.1 78.1 %all-to-all-start = ((bf16[16,128,768]{2,1,0:T(8,128)(2,1)}), bf16[16,128,768]{2,1,0:T(8,128)(2,1)}, u32[]{:S(2)}, u32[]{:S(2)}) async-start(bf16[16,128,768]{2,1,0:T(8,128)(2,1)} %broadcast_select_fusion.6), calls=%async_computation | async-start | bytes 6291456 | tf_op jit(solution)/shard_map/all_to_all | solution.py:206
  25.4 1501.8 %all-reduce.23.cloned.1.call-start = ((), (), s32[]{:S(2)}) async-start(), calls=%async_computation.6 | async-start | bytes 30146560
  27.1 97.1 %copy-start.59 = (pred[1024]{0:T(1024)(128)(4,1)}, pred[1024]{0:T(1024)(128)(4,1)S(1)}, u32[]{:S(2)}) copy-start(pred[1024]{0:T(1024)(128)(4,1)S(1)} %get-tuple-element.907) | copy-start | bytes 3076
  27.1 114.3 %copy-start.32 = (f32[1024]{0:T(1024)}, f32[1024]{0:T(1024)S(1)}, u32[]{:S(2)}) copy-start(f32[1024]{0:T(1024)S(1)} %get-tuple-element.908) | copy-start | bytes 12292
  27.2 114.2 %copy-start.34 = (f32[1,1024]{1,0:T(1,128)}, f32[1,1024]{1,0:T(1,128)S(1)}, u32[]{:S(2)}) copy-start(f32[1,1024]{1,0:T(1,128)S(1)} %get-tuple-element.896) | copy-start | bytes 12292
  27.2 114.2 %copy-start.36 = (f32[1,1024]{1,0:T(1,128)}, f32[1,1024]{1,0:T(1,128)S(1)}, u32[]{:S(2)}) copy-start(f32[1,1024]{1,0:T(1,128)S(1)} %get-tuple-element.897) | copy-start | bytes 12292
  27.2 114.2 %copy-start.38 = (f32[1,1024]{1,0:T(1,128)}, f32[1,1024]{1,0:T(1,128)S(1)}, u32[]{:S(2)}) copy-start(f32[1,1024]{1,0:T(1,128)S(1)} %get-tuple-element.898) | copy-start | bytes 12292
  106.8 17.3 copy-start.8
  107.5 16.0 copy-start.42
  107.5 16.6 copy-start.49
  442.7 24.5 %copy-start.22 = (f32[1536]{0:T(1024)}, f32[1536]{0:T(1024)S(1)}, u32[]{:S(2)}) copy-start(f32[1536]{0:T(1024)S(1)} %mul.958) | copy-start | bytes 18436
  453.1 14.0 copy-start.53
  498.3 14.7 copy-start.40
  533.5 11.8 copy-start.7
  533.5 11.8 copy-start.10
  533.5 13.9 copy-start.3
  578.0 44.8 %copy-start.17 = (f32[256,24]{0,1:T(8,128)S(1)}, f32[256,24]{0,1:T(8,128)}, u32[]{:S(2)}) copy-start(f32[256,24]{0,1:T(8,128)} %copy.391) | copy-start | bytes 73732 | tf_op jit(solution)/shard_map/transpose(jvp())/while
  585.2 39.9 %copy-start.56 = (f32[24]{0:T(128)S(1)}, f32[24]{0:T(128)}, u32[]{:S(2)}) copy-start(f32[24]{0:T(128)} %get-tuple-element.1213) | copy-start | bytes 292 | tf_op jit(solution)/shard_map/transpose(jvp())/while
  585.2 40.5 %copy-start.15 = (f32[4,1,256,128]{3,2,1,0:T(8,128)S(1)}, f32[4,1,256,128]{3,2,1,0:T(8,128)}, u32[]{:S(2)}) copy-start(f32[4,1,256,128]{3,2,1,0:T(8,128)} %copy-done.14) | copy-start | bytes 1572868 | tf_op jit(solution)/shard_map/transpose(jvp())/while
  585.2 40.5 %copy-start.41 = (f32[24]{0:T(128)S(1)}, f32[24]{0:T(128)}, u32[]{:S(2)}) copy-start(f32[24]{0:T(128)} %copy-done.40) | copy-start | bytes 292 | tf_op jit(solution)/shard_map/transpose(jvp())/while
  625.7 15.8 copy-start.40
  662.1 11.8 copy-start.7
  662.1 11.8 copy-start.10
  662.1 13.9 copy-start.3
  706.5 44.8 %copy-start.17 = (f32[256,24]{0,1:T(8,128)S(1)}, f32[256,24]{0,1:T(8,128)}, u32[]{:S(2)}) copy-start(f32[256,24]{0,1:T(8,128)} %copy.391) | copy-start | bytes 73732 | tf_op jit(solution)/shard_map/transpose(jvp())/while
  713.7 39.9 %copy-start.56 = (f32[24]{0:T(128)S(1)}, f32[24]{0:T(128)}, u32[]{:S(2)}) copy-start(f32[24]{0:T(128)} %get-tuple-element.1213) | copy-start | bytes 292 | tf_op jit(solution)/shard_map/transpose(jvp())/while
  713.7 40.5 %copy-start.15 = (f32[4,1,256,128]{3,2,1,0:T(8,128)S(1)}, f32[4,1,256,128]{3,2,1,0:T(8,128)}, u32[]{:S(2)}) copy-start(f32[4,1,256,128]{3,2,1,0:T(8,128)} %copy-done.14) | copy-start | bytes 1572868 | tf_op jit(solution)/shard_map/transpose(jvp())/while
  713.7 40.5 %copy-start.41 = (f32[24]{0:T(128)S(1)}, f32[24]{0:T(128)}, u32[]{:S(2)}) copy-start(f32[24]{0:T(128)} %copy-done.40) | copy-start | bytes 292 | tf_op jit(solution)/shard_map/transpose(jvp())/while
  754.2 15.9 copy-start.40
  790.7 11.8 copy-start.7
  790.7 11.8 copy-start.10
  790.7 13.9 copy-start.3
  835.1 44.8 %copy-start.17 = (f32[256,24]{0,1:T(8,128)S(1)}, f32[256,24]{0,1:T(8,128)}, u32[]{:S(2)}) copy-start(f32[256,24]{0,1:T(8,128)} %copy.391) | copy-start | bytes 73732 | tf_op jit(solution)/shard_map/transpose(jvp())/while
  842.3 39.9 %copy-start.56 = (f32[24]{0:T(128)S(1)}, f32[24]{0:T(128)}, u32[]{:S(2)}) copy-start(f32[24]{0:T(128)} %get-tuple-element.1213) | copy-start | bytes 292 | tf_op jit(solution)/shard_map/transpose(jvp())/while
  842.3 40.5 %copy-start.15 = (f32[4,1,256,128]{3,2,1,0:T(8,128)S(1)}, f32[4,1,256,128]{3,2,1,0:T(8,128)}, u32[]{:S(2)}) copy-start(f32[4,1,256,128]{3,2,1,0:T(8,128)} %copy-done.14) | copy-start | bytes 1572868 | tf_op jit(solution)/shard_map/transpose(jvp())/while
  842.3 40.5 %copy-start.41 = (f32[24]{0:T(128)S(1)}, f32[24]{0:T(128)}, u32[]{:S(2)}) copy-start(f32[24]{0:T(128)} %copy-done.40) | copy-start | bytes 292 | tf_op jit(solution)/shard_map/transpose(jvp())/while
  882.8 15.9 copy-start.40
  919.3 11.8 copy-start.7
  919.3 11.8 copy-start.10
  919.3 13.9 copy-start.3
  963.8 44.8 %copy-start.17 = (f32[256,24]{0,1:T(8,128)S(1)}, f32[256,24]{0,1:T(8,128)}, u32[]{:S(2)}) copy-start(f32[256,24]{0,1:T(8,128)} %copy.391) | copy-start | bytes 73732 | tf_op jit(solution)/shard_map/transpose(jvp())/while
  970.9 39.9 %copy-start.56 = (f32[24]{0:T(128)S(1)}, f32[24]{0:T(128)}, u32[]{:S(2)}) copy-start(f32[24]{0:T(128)} %get-tuple-element.1213) | copy-start | bytes 292 | tf_op jit(solution)/shard_map/transpose(jvp())/while
  971.0 40.5 %copy-start.15 = (f32[4,1,256,128]{3,2,1,0:T(8,128)S(1)}, f32[4,1,256,128]{3,2,1,0:T(8,128)}, u32[]{:S(2)}) copy-start(f32[4,1,256,128]{3,2,1,0:T(8,128)} %copy-done.14) | copy-start | bytes 1572868 | tf_op jit(solution)/shard_map/transpose(jvp())/while
  971.0 40.5 %copy-start.41 = (f32[24]{0:T(128)S(1)}, f32[24]{0:T(128)}, u32[]{:S(2)}) copy-start(f32[24]{0:T(128)} %copy-done.40) | copy-start | bytes 292 | tf_op jit(solution)/shard_map/transpose(jvp())/while
  1028.4 19.7 copy-start.25
  1028.4 19.7 copy-start.27
  1028.4 19.7 copy-start.29
  1028.4 19.7 copy-start.31
  1060.0 15.1 copy-start.9
  1060.0 15.1 copy-start.50
  1060.0 15.1 copy-start.52
  1060.0 15.1 copy-start.60
  1089.6 12.5 copy-start.21
  1089.6 12.5 copy-start.45
  1089.6 12.5 copy-start.54
  1128.2 91.9 %copy-start.58 = (f32[24]{0:T(128)S(1)}, f32[24]{0:T(128)}, u32[]{:S(2)}) copy-start(f32[24]{0:T(128)} %get-tuple-element.474) | copy-start | bytes 292
  1128.2 95.3 %copy-start.61 = (f32[1536]{0:T(1024)S(1)}, f32[1536]{0:T(1024)}, u32[]{:S(2)}) copy-start(f32[1536]{0:T(1024)} %get-tuple-element.783) | copy-start | bytes 18436
  1267.1 265.1 %copy-start.64 = (f32[2]{0:T(128)S(1)}, f32[2]{0:T(128)}, u32[]{:S(2)}) copy-start(f32[2]{0:T(128)} %param.24) | copy-start | bytes 28
  1267.1 838.6 %all-gather.9.cloned.1.call-start = ((), (), s32[]{:S(2)}) async-start(), calls=%async_computation.5 | async-start | bytes 33914880 | tf_op jit(solution)/shard_map/all_gather | solution.py:290
  1531.4 863.5 %all-gather.7.cloned.1.call-start = ((), (), s32[]{:S(2)}) async-start(), calls=%async_computation.4 | async-start | bytes 18841600 | tf_op jit(solution)/shard_map/all_gather | solution.py:294
  2229.0 75.9 %all-to-all-start.1 = ((bf16[2,1024,768]{2,0,1:T(2,128)(2,1)}), bf16[2,1024,768]{2,0,1:T(2,128)(2,1)}, u32[]{:S(2)}, u32[]{:S(2)}) async-start(bf16[2,1024,768]{2,0,1:T(2,128)(2,1)} %copy.241), calls=%async_computation.1 | async-start | bytes 6291456 | tf_op jit(solution)/shard_map/all_to_all | solution.py:268
  2233.8 74.7 %copy-start.55 = (s32[8,2]{1,0:T(8,128)S(1)}, s32[8,2]{1,0:T(8,128)}, u32[]{:S(2)}) copy-start(s32[8,2]{1,0:T(8,128)} %get-tuple-element.789) | copy-start | bytes 196
  2304.8 74.5 %all-to-all-start.2 = ((bf16[2,1024,768]{2,0,1:T(2,128)(2,1)}), bf16[2,1024,768]{2,0,1:T(2,128)(2,1)S(1)}, u32[]{:S(2)}, u32[]{:S(2)}) async-start(bf16[2,1024,768]{2,0,1:T(2,128)(2,1)} %copy.255), calls=%async_computation.2 | async-start | bytes 6291456 | tf_op jit(solution)/shard_map/all_to_all | solution.py:269
  (43 other events, 259.5 us)
Sparse Core Ops, SparseCore 0:
  11.0 56.1 all-gather.4
  1267.2 259.9 all-reduce.22
  1531.5 574.0 all-gather.8
  2186.7 96.2 all-gather.6
